TPU v7x, 32 devices: a whole 2x2x4 slice. The times are simulated.
32 devices in a mesh: seq: 8 (over z, x), dp: 4 (over y, core).
Axes of the slice: x: 2, y: 2, z: 4, core: 2. Of those that a mesh axis runs over, the one named last changes fastest.
Arguments:
- conv_input: bfloat16 [4, 2048, 2816], P('dp', 'seq'), may hold values from -6 to 6
- gate_input: bfloat16 [4, 2048, 2560], P('dp', 'seq'), may hold values from -6 to 6
- step_input: float32 [4, 40, 2048], P('dp', None, 'seq'), may hold values from -7.5 to 2048
- filter_taps: float32 [4, 2816], replicated, may hold values from -3 to 3
- filter_bias: float32 [2816], replicated, may hold values from -0.5 to 0.5
- step_bias: float32 [40], replicated, may hold values from -1 to 1
- decay_log: float32 [40], replicated, may hold values from -13 to 3
- skip_gain: float32 [40], replicated, may hold values from 0.5 to 1.5
- norm_weight: float32 [2560], replicated, may hold values from 0.5 to 1.5
- output_weight: bfloat16 [2560, 1280], P('dp'), may hold values from -0.125 to 0.125
- output_grad: bfloat16 [4, 2048, 1280], P('dp', 'seq'), may hold values from -6 to 6
Outputs:
- input_grad: bfloat16 [4, 2048, 2816], P('dp', 'seq')
- gate_grad: bfloat16 [4, 2048, 2560], P('dp', 'seq')
- step_grad: float32 [4, 40, 2048], P('dp', None, 'seq')
- weight_grad: float32 [2560, 1280], P('dp')
- filter_grads: float32 [5, 2816], replicated
- norm_grad: float32 [2560], replicated
- head_grads: float32 [3, 40], replicated
All inputs are finite; a program needn't handle non-finite values.
Results may differ from a plain program's by a relative error of at most 0.0029.
Values may be sent and summed in bfloat16 or wider, within the bound.
A program may use at most 192 MiB of HBM per device.

v0:
```python
import jax
import jax.numpy as jnp
from jax import lax
from jax.sharding import PartitionSpec as P

HEADS = 40
HEAD_DIM = 64
STATE = 128
SPAN = 256
INNER = 2560
PRECISE = lax.Precision.HIGH
MASKED = -1e30
EPSILON = 1e-05


def passed_along(value, axis, steps):
    count = lax.axis_size(axis)
    first, last = (max(0, -steps), min(count, count - steps))
    return lax.ppermute(value, axis, [(source, source + steps) for source in range(first, last)])


def spread(table, axis):
    count = lax.axis_size(axis)
    return lax.all_to_all(
        jnp.broadcast_to(table[None], (count,) + table.shape),
        axis,
        split_axis=0,
        concat_axis=0,
        tiled=True,
    )


def carried(states, decay_table, axis, reverse):
    count = lax.axis_size(axis)
    heads, features, width = states.shape
    pieces = states.reshape(heads, count, features // count, width).transpose(1, 0, 2, 3)
    pieces = lax.all_to_all(pieces, axis, split_axis=0, concat_axis=0, tiled=True)
    running = jnp.zeros(pieces.shape[1:], jnp.float32)
    found = [None] * count
    for at in reversed(range(count)) if reverse else range(count):
        found[at] = running
        running = decay_table[at][:, None, None] * running + pieces[at]
    back = lax.all_to_all(jnp.stack(found), axis, split_axis=0, concat_axis=0, tiled=True)
    return back.transpose(1, 0, 2, 3).reshape(heads, features, width)


def summed_everywhere(parts, axes):
    count = 1
    for axis in axes:
        count = count * lax.axis_size(axis)
    flat = jnp.concatenate([part.reshape(-1) for part in parts])
    chunk = -(-flat.shape[0] // (count * 128)) * 128
    padded = jnp.pad(flat, (0, chunk * count - flat.shape[0])).reshape(count, chunk)
    terms = lax.all_to_all(padded, axes, split_axis=0, concat_axis=0, tiled=True)
    total = lax.all_gather(jnp.sum(terms, axis=0), axes, axis=0, tiled=True)
    results, start = ([], 0)
    for part in parts:
        results.append(total[start : start + part.size].reshape(part.shape))
        start += part.size
    return results


def prepare(extended, step_rows, filter_taps, filter_bias, step_bias, decay_log):
    width = filter_taps.shape[0]
    length = extended.shape[0] - width + 1
    filtered = filter_bias + filter_taps[0] * extended[0:length]
    for offset in range(1, width):
        filtered = filtered + filter_taps[offset] * extended[offset : offset + length]
    activated = jax.nn.silu(filtered)
    step_sizes = jax.nn.softplus(step_rows + step_bias[:, None])
    decay_rates = step_sizes * (-jnp.exp(decay_log))[:, None]
    blocks = length // SPAN
    cumsums = jnp.cumsum(decay_rates.reshape(HEADS, blocks, SPAN), axis=2)
    values = activated[:, :INNER].reshape(blocks, SPAN, HEADS, HEAD_DIM)
    key_side = activated[:, INNER : INNER + STATE].reshape(blocks, SPAN, STATE)
    scaled = values * step_sizes.reshape(HEADS, blocks, SPAN).transpose(1, 2, 0)[..., None]
    to_end = jnp.exp(cumsums[:, :, -1:] - cumsums)
    block_states = jnp.einsum("hcs,cshp,csn->chpn", to_end, scaled, key_side, precision=PRECISE)
    decays = jnp.exp(cumsums[:, :, -1]).T
    return (activated, cumsums, scaled, block_states, decays)


def finish(
    activated, cumsums, scaled, block_states, decays, entering, skip_gain, gate_rows, norm_weight
):
    blocks = cumsums.shape[1]
    length = blocks * SPAN
    values = activated[:, :INNER].reshape(blocks, SPAN, HEADS, HEAD_DIM)
    key_side = activated[:, INNER : INNER + STATE].reshape(blocks, SPAN, STATE)
    query_side = activated[:, INNER + STATE :].reshape(blocks, SPAN, STATE)
    starting = []
    starting.append(entering)
    starting = jnp.stack(starting)
    scores = jnp.einsum("ctn,csn->cts", query_side, key_side, precision=PRECISE)
    differences = cumsums[:, :, :, None] - cumsums[:, :, None, :]
    causal = jnp.tril(jnp.ones((SPAN, SPAN), dtype=bool))
    weights = scores[None] * jnp.exp(jnp.where(causal, differences, MASKED))
    inside = jnp.einsum("hcts,cshp->cthp", weights, scaled, precision=PRECISE)
    from_state = (
        jnp.einsum("ctn,chpn->cthp", query_side, starting, precision=PRECISE)
        * jnp.exp(cumsums).transpose(1, 2, 0)[..., None]
    )
    result = inside + from_state + skip_gain[:, None] * values
    scanned = result.reshape(length, INNER)
    gated = scanned * jax.nn.silu(gate_rows)
    inverse_rms = lax.rsqrt(jnp.mean(gated * gated, axis=1, keepdims=True) + EPSILON)
    return gated * inverse_rms * norm_weight


def body(
    conv_input,
    gate_input,
    step_input,
    filter_taps,
    filter_bias,
    step_bias,
    decay_log,
    skip_gain,
    norm_weight,
    output_weight,
    output_grad,
):
    kernel_rows = filter_taps.shape[0] - 1
    raw_rows = conv_input[0]
    before = passed_along(raw_rows[-kernel_rows:], "seq", 1)
    extended = jnp.concatenate([before, raw_rows], axis=0).astype(jnp.float32)
    gate_rows = gate_input[0].astype(jnp.float32)
    step_rows = step_input[0]
    cotangent = output_grad[0]
    tokens = cotangent.shape[0]
    primals, pull_first = jax.vjp(
        prepare, extended, step_rows, filter_taps, filter_bias, step_bias, decay_log
    )
    activated, cumsums, scaled, block_states, decays = primals
    decay_table = spread(decays[0], "seq")
    entering = carried(block_states[0], decay_table, "seq", False)
    normed, pull_second = jax.vjp(
        finish,
        activated,
        cumsums,
        scaled,
        block_states,
        decays,
        entering,
        skip_gain,
        gate_rows,
        norm_weight,
    )
    normed_low = normed.astype(jnp.bfloat16)
    groups = lax.axis_size("dp")
    own_rows = output_weight.shape[0]
    everyone = lax.all_gather(cotangent, "dp", axis=0, tiled=True)
    partial_columns = lax.dot_general(
        everyone, output_weight, (((1,), (1,)), ((), ())), preferred_element_type=jnp.float32
    )
    regrouped = partial_columns.reshape(groups, tokens, own_rows)
    normed_grad = lax.all_to_all(regrouped, "dp", split_axis=0, concat_axis=2, tiled=True).reshape(
        tokens, groups * own_rows
    )
    own_columns = lax.all_to_all(normed_low, "dp", split_axis=1, concat_axis=0, tiled=True)
    weight_piece = lax.dot_general(
        own_columns, everyone, (((0,), (0,)), ((), ())), preferred_element_type=jnp.float32
    )
    spans = lax.axis_size("seq")
    weight_terms = lax.all_to_all(
        weight_piece.astype(jnp.bfloat16).reshape(spans, own_rows // spans, -1),
        "seq",
        split_axis=0,
        concat_axis=0,
        tiled=True,
    )
    weight_rows = jnp.sum(weight_terms.astype(jnp.float32), axis=0)
    weight_grad = lax.all_gather(weight_rows, "seq", axis=0, tiled=True)
    second = pull_second(normed_grad)
    (
        grad_activated,
        grad_cumsums,
        grad_scaled,
        grad_states,
        grad_decays,
        grad_entering,
        grad_skip,
        grad_gate,
        grad_norm,
    ) = second
    end_grad = carried(grad_entering, decay_table, "seq", True)
    decay_grad = jnp.sum(end_grad * entering, axis=(1, 2))
    first = pull_first(
        (
            grad_activated,
            grad_cumsums,
            grad_scaled,
            grad_states + end_grad[None],
            grad_decays + decay_grad[None],
        )
    )
    grad_extended, grad_steps, grad_taps, grad_bias, grad_step_bias, grad_decay_log = first
    returned = passed_along(grad_extended[:kernel_rows], "seq", -1)
    own_part = grad_extended[kernel_rows:]
    own_part = jnp.concatenate(
        [own_part[:-kernel_rows], own_part[-kernel_rows:] + returned], axis=0
    )
    filter_part = jnp.concatenate([grad_taps, grad_bias[None]], axis=0)
    head_part = jnp.stack([grad_step_bias, grad_decay_log, grad_skip])
    filter_grads, norm_grad, head_grads = summed_everywhere(
        (filter_part, grad_norm, head_part), ("seq", "dp")
    )
    input_grad = own_part.astype(jnp.bfloat16)[None]
    gate_grad = grad_gate.astype(jnp.bfloat16)[None]
    step_grad = grad_steps[None]
    return (input_grad, gate_grad, step_grad, weight_grad, filter_grads, norm_grad, head_grads)


def solution(mesh):
    return jax.shard_map(
        body,
        mesh=mesh,
        in_specs=(
            P("dp", "seq", None),
            P("dp", "seq", None),
            P("dp", None, "seq"),
            P(),
            P(),
            P(),
            P(),
            P(),
            P(),
            P("dp", None),
            P("dp", "seq", None),
        ),
        out_specs=(
            P("dp", "seq", None),
            P("dp", "seq", None),
            P("dp", None, "seq"),
            P("dp", None),
            P(),
            P(),
            P(),
        ),
        check_vma=False,
    )
```

profile of v0, /device:TPU:0, one launch (start us, length us, event | category | flops | bytes accessed | tf_op | source)
XLA Modules:
  0.0 410.9 jit_solution(12304909783855509701)
XLA Ops:
  8.1 4.9 %collective-permute-start = (bf16[3,2816]{1,0:T(4,128)(2,1)S(1)}, bf16[3,2816]{1,0:T(4,128)(2,1)S(1)}, u32[]{:S(2)}, u32[]{:S(2)}) collective-permute-start(bf16[3,2816]{1,0:T(4,128)(2,1)S(1)} %slice_bitcast_fusion), channel_id=1, source_target_pairs={{0,4},{4,8},{8,12},{12,16},{16,20},{20,24},{24,28},{1,5},{5,9},{9,... | collective-permute-start | bytes 50696 | tf_op jit(solution)/shard_map/ppermute | solution.py:19
  16.9 4.9 %all-to-all-start.1 = ((f32[8,1,40]{2,1,0:T(1,128)}), f32[8,1,40]{2,1,0:T(1,128)S(1)}, u32[]{:S(2)}, u32[]{:S(2)}) async-start(f32[8,1,40]{2,1,0:T(1,128)} %broadcast_in_dim.32), calls=%async_computation.1 | async-start | bytes 8192 | tf_op jit(solution)/shard_map/all_to_all | solution.py:24
  41.1 6.0 %all-to-all-start.2 = ((f32[8,40,8,128]{3,2,1,0:T(8,128)}), f32[8,40,8,128]{3,2,1,0:T(8,128)S(1)}, u32[]{:S(2)}, u32[]{:S(2)}) async-start(f32[8,40,8,128]{3,2,1,0:T(8,128)} %copy.225), calls=%async_computation.2 | async-start | bytes 2621440 | tf_op jit(solution)/shard_map/all_to_all | solution.py:37
  49.9 28.0 %all-to-all-done.2 = f32[8,40,8,128]{3,2,1,0:T(8,128)S(1)} async-done(((f32[8,40,8,128]{3,2,1,0:T(8,128)}), f32[8,40,8,128]{3,2,1,0:T(8,128)S(1)}, u32[]{:S(2)}, u32[]{:S(2)}) %all-to-all-start.2) | async-done | bytes 1310752 | tf_op jit(solution)/shard_map/all_to_all | solution.py:37
  87.1 5.5 %fusion.44 = f32[1024,640]{1,0:T(8,128)} fusion(bf16[640,1280]{1,0:T(8,128)(2,1)S(1)} %copy-done, bf16[1,1024,1280]{2,1,0:T(8,128)(2,1)} %all-gather.7.cloned.1.call-done), kind=kOutput, calls=%fused_computation.67 | convolution fusion | flops 1677721600 | bytes 6881280 | tf_op jit(solution)/shard_map/dot_general | solution.py:153
  92.6 25.8 %all-to-all-done.3 = f32[8,40,8,128]{3,2,1,0:T(8,128)S(1)} async-done(((f32[8,40,8,128]{3,2,1,0:T(8,128)}), f32[8,40,8,128]{3,2,1,0:T(8,128)S(1)}, u32[]{:S(2)}, u32[]{:S(2)}) %all-to-all-start.3) | async-done | bytes 1310752 | tf_op jit(solution)/shard_map/all_to_all | solution.py:43
  134.4 20.4 %all-to-all-done = f32[4,256,640]{2,1,0:T(8,128)S(1)} async-done(((f32[4,256,640]{2,1,0:T(8,128)}), f32[4,256,640]{2,1,0:T(8,128)S(1)}, u32[]{:S(2)}, u32[]{:S(2)}) %all-to-all-start) | async-done | bytes 2621472 | tf_op jit(solution)/shard_map/all_to_all | solution.py:157
  157.3 10.1 %multiply_reduce_fusion.9 = (f32[256]{0:T(256)S(1)}, f32[256]{0:T(256)S(1)}, f32[1,256,40,64]{1,3,2,0:T(8,128)S(1)}) fusion(f32[1,256,40,64]{1,3,2,0:T(8,128)} %bitcast.317, f32[1,256,40,64]{1,3,2,0:T(8,128)} %bitcast.329, f32[40,64]{1,0:T(8,128)S(1)} %mul.692, f32[1,256,40,64]{1,3,2,0:T(8,128)} %bitcast.323, f32[40]{0:T(128)S(1)} %copy-done.51, ...), kind=kOutput, calls=%fused_computation.74 | convolution fusion | flops 1024327168 | bytes 16191648 | tf_op jit(solution)/shard_map/jvp(hcts,cshp->cthp)/dot_general | solution.py:98
  169.4 4.3 %all-to-all-start.6 = ((bf16[256,4,640]{0,2,1:T(8,128)(2,1)}), bf16[256,4,640]{0,2,1:T(8,128)(2,1)}, u32[]{:S(2)}, u32[]{:S(2)}) async-start(bf16[256,4,640]{0,2,1:T(8,128)(2,1)} %multiply_convert_fusion), calls=%async_computation.6 | async-start | bytes 2621440 | tf_op jit(solution)/shard_map/all_to_all | solution.py:160
  173.7 4.2 %broadcast_multiply_fusion.5 = (f32[1,256,40,64]{1,3,2,0:T(8,128)}, f32[1,256,40,64]{1,3,2,0:T(8,128)S(1)}) fusion(f32[40]{0:T(128)S(1)} %copy-done.51, f32[256]{0:T(256)S(1)} %get-tuple-element.107, f32[1,256,40,64]{1,3,2,0:T(8,128)S(1)} %get-tuple-element.108, f32[1,256,40,64]{1,3,2,0:T(8,128)} %bitcast.318, f32[256]{0:T(256)S(1)} %get-tuple-element.106, ...), kind=kLoop, calls=%fused_computation.104 | loop fusion | flops 7864320 | bytes 13119648 | tf_op jit(solution)/shard_map/transpose(jvp())/mul | solution.py:103
  182.7 8.2 %all-to-all-done.6 = bf16[256,4,640]{0,2,1:T(8,128)(2,1)} async-done(((bf16[256,4,640]{0,2,1:T(8,128)(2,1)}), bf16[256,4,640]{0,2,1:T(8,128)(2,1)}, u32[]{:S(2)}, u32[]{:S(2)}) %all-to-all-start.6) | async-done | bytes 1310752 | tf_op jit(solution)/shard_map/all_to_all | solution.py:160
  191.0 4.3 %all-to-all-start.4 = ((f32[8,40,8,128]{3,2,1,0:T(8,128)}), f32[8,40,8,128]{3,2,1,0:T(8,128)}, u32[]{:S(2)}, u32[]{:S(2)}) async-start(f32[8,40,8,128]{3,2,1,0:T(8,128)} %copy.232), calls=%async_computation.4 | async-start | bytes 2621440 | tf_op jit(solution)/shard_map/all_to_all | solution.py:37
  200.9 5.3 %convolution_convert_fusion = bf16[640,1280]{1,0:T(8,128)(2,1)} fusion(bf16[1024,640]{1,0:T(8,128)(2,1)} %bitcast.342, bf16[1,1024,1280]{2,1,0:T(8,128)(2,1)} %all-gather.7.cloned.1.call-done), kind=kOutput, calls=%fused_computation.24 | convolution fusion | flops 1678540800 | bytes 5570560 | tf_op jit(solution)/shard_map/dot_general | solution.py:161
  206.2 20.4 %all-to-all-done.4 = f32[8,40,8,128]{3,2,1,0:T(8,128)} async-done(((f32[8,40,8,128]{3,2,1,0:T(8,128)}), f32[8,40,8,128]{3,2,1,0:T(8,128)}, u32[]{:S(2)}, u32[]{:S(2)}) %all-to-all-start.4) | async-done | bytes 1310752 | tf_op jit(solution)/shard_map/all_to_all | solution.py:37
  226.6 4.5 %all-to-all-start.7 = ((bf16[8,80,1280]{2,1,0:T(8,128)(2,1)}), bf16[8,80,1280]{2,1,0:T(8,128)(2,1)}, u32[]{:S(2)}, u32[]{:S(2)}) async-start(bf16[8,80,1280]{2,1,0:T(8,128)(2,1)} %bitcast.340), calls=%async_computation.7 | async-start | bytes 3276800 | tf_op jit(solution)/shard_map/all_to_all | solution.py:165
  231.1 4.3 %fusion.24 = bf16[1,256,2560]{1,2,0:T(8,128)(2,1)} fusion(f32[1,256,4,640]{1,3,2,0:T(8,128)} %copy.218, f32[1,256,40,64]{1,3,2,0:T(8,128)S(1)} %get-tuple-element.108, f32[256]{0:T(256)S(1)} %get-tuple-element.107, f32[256]{0:T(256)S(1)} %get-tuple-element.106, f32[2560]{0:T(1024)S(1)} %copy-done.25, bf16[1,256,2560]{1,2,0:T(8,128)(2,1)} %copy.229), kind=kLoop, calls=%fused_computation.40 | loop fusion | flops 12451840 | bytes 7876608 | tf_op jit(solution)/shard_map/convert_element_type | solution.py:209
  256.0 13.1 %all-to-all-done.7 = bf16[8,80,1280]{2,1,0:T(8,128)(2,1)} async-done(((bf16[8,80,1280]{2,1,0:T(8,128)(2,1)}), bf16[8,80,1280]{2,1,0:T(8,128)(2,1)}, u32[]{:S(2)}, u32[]{:S(2)}) %all-to-all-start.7) | async-done | bytes 1638432 | tf_op jit(solution)/shard_map/all_to_all | solution.py:165
  269.1 4.3 %all-to-all-start.5 = ((f32[8,40,8,128]{3,2,1,0:T(8,128)}), f32[8,40,8,128]{3,2,1,0:T(8,128)}, u32[]{:S(2)}, u32[]{:S(2)}) async-start(f32[8,40,8,128]{3,2,1,0:T(8,128)} %broadcast_dynamic-update-slice_fusion), calls=%async_computation.5 | async-start | bytes 2621440 | tf_op jit(solution)/shard_map/all_to_all | solution.py:43
  273.5 13.1 %fusion.6 = (f32[40,256]{1,0:T(8,128)}, f32[40,256]{1,0:T(8,128)S(1)}, f32[256,256]{1,0:T(8,128)S(1)}) fusion(f32[40,256]{1,0:T(8,128)} %get-tuple-element.88, f32[256,256]{1,0:T(8,128)S(1)} %copy-done.17, pred[256,256]{1,0:T(8,128)(4,1)} %copy-done.26, f32[256,40,64]{0,2,1:T(8,128)} %bitcast.325, f32[256,40]{0,1:T(8,128)S(1)} %fusion.124, ...), kind=kOutput, calls=%fused_computation.7 | convolution fusion | flops 1030795264 | bytes 5996544 | tf_op jit(solution)/shard_map/transpose(jvp(hcts,cshp->cthp))/dot_general | solution.py:98
  291.0 4.4 %multiply_reduce_fusion.6 = f32[4,640]{1,0:T(4,128)S(1)} fusion(f32[1,256,4,640]{3,1,2,0:T(8,128)} %copy.248, f32[1,256,4,640]{3,1,2,0:T(8,128)} %copy.247, f32[256]{0:T(256)S(1)} %copy-done.31, f32[4,256,640]{2,1,0:T(8,128)} %copy-done.6), kind=kLoop, calls=%fused_computation.70 | loop fusion | flops 5240320 | bytes 7875584 | tf_op jit(solution)/shard_map/transpose(jvp())/reduce_sum | solution.py:107
  311.5 7.5 %multiply_reduce_fusion.5 = (f32[40]{0:T(128)}, f32[256,40]{0,1:T(8,128)}, f32[1,256,40,64]{1,3,2,0:T(8,128)}) fusion(f32[1,256,40,64]{1,3,2,0:T(8,128)S(1)} %copy-done.9, f32[1,256,40,64]{1,3,2,0:T(8,128)S(1)} %bitcast.327, f32[256,40]{0,1:T(8,128)S(1)} %fusion.124, f32[256,40]{0,1:T(8,128)S(1)} %get-tuple-element.87, ...), kind=kOutput, calls=%fused_computation.69 | convolution fusion | flops 1019074560 | bytes 10977440 | tf_op jit(solution)/shard_map/transpose(jvp(hcts,cshp->cthp))/dot_general | solution.py:98
  325.9 5.4 %multiply_reduce_fusion.4 = (f32[2816]{0:T(1024)S(1)}, f32[2816]{0:T(1024)S(1)}, f32[2816]{0:T(1024)S(1)}, f32[2816]{0:T(1024)S(1)}, f32[2816]{0:T(1024)}, /*index=5*/f32[256,2816]{1,0:T(8,128)S(1)}) fusion(f32[259,2816]{1,0:T(8,128)S(1)} %copy-done.3, f32[256,2816]{1,0:T(8,128)} %get-tuple-element.90, f32[256,2560]{1,0:T(8,128)} %copy.235, ...), kind=kLoop, calls=%fused_computation.32 | loop fusion | flops 15845632 | bytes 22993920 | tf_op jit(solution)/shard_map/transpose(jvp())/reduce_sum | solution.py:68
  343.5 5.1 %all-to-all-start.8 = ((f32[32,1,640]{2,1,0:T(1,128)}), f32[32,1,640]{2,1,0:T(1,128)S(1)}, u32[]{:S(2)}, u32[]{:S(2)}) async-start(f32[32,1,640]{2,1,0:T(1,128)} %bitcast.102), calls=%async_computation.8 | async-start | bytes 163840 | tf_op jit(solution)/shard_map/all_to_all | solution.py:54
  357.9 40.0 %all-gather.1 = f32[32,1,640]{2,1,0:T(1,128)S(1)} all-gather(f32[1,1,640]{2,1,0:T(1,128)S(1)} %reshape.1035), channel_id=1, replica_groups=mesh['seq'=8,'dp'=4] {'seq','dp'}, dimensions={0}, use_global_device_ids=true | all-gather | bytes 84480 | tf_op jit(solution)/shard_map/all_gather | solution.py:55
  (236 shorter events, 141.9 us)
Async XLA Ops:
  7.2 79.9 %copy-start = (bf16[640,1280]{1,0:T(8,128)(2,1)S(1)}, bf16[640,1280]{1,0:T(8,128)(2,1)}, u32[]{:S(2)}) copy-start(bf16[640,1280]{1,0:T(8,128)(2,1)} %param.20) | copy-start | bytes 4915204
  8.1 16.8 %collective-permute-start = (bf16[3,2816]{1,0:T(4,128)(2,1)S(1)}, bf16[3,2816]{1,0:T(4,128)(2,1)S(1)}, u32[]{:S(2)}, u32[]{:S(2)}) collective-permute-start(bf16[3,2816]{1,0:T(4,128)(2,1)S(1)} %slice_bitcast_fusion), channel_id=1, source_target_pairs={{0,4},{4,8},{8,12},{12,16},{16,20},{20,24},{24,28},{1,5},{5,9},{9,... | collective-permute-start | bytes 50696 | tf_op jit(solution)/shard_map/ppermute | solution.py:19
  16.9 23.6 %all-to-all-start.1 = ((f32[8,1,40]{2,1,0:T(1,128)}), f32[8,1,40]{2,1,0:T(1,128)S(1)}, u32[]{:S(2)}, u32[]{:S(2)}) async-start(f32[8,1,40]{2,1,0:T(1,128)} %broadcast_in_dim.32), calls=%async_computation.1 | async-start | bytes 8192 | tf_op jit(solution)/shard_map/all_to_all | solution.py:24
  41.1 36.8 %all-to-all-start.2 = ((f32[8,40,8,128]{3,2,1,0:T(8,128)}), f32[8,40,8,128]{3,2,1,0:T(8,128)S(1)}, u32[]{:S(2)}, u32[]{:S(2)}) async-start(f32[8,40,8,128]{3,2,1,0:T(8,128)} %copy.225), calls=%async_computation.2 | async-start | bytes 2621440 | tf_op jit(solution)/shard_map/all_to_all | solution.py:37
  47.1 40.0 %all-gather.7.cloned.1.call-start = ((), (), s32[]{:S(2)}) async-start(), calls=%async_computation.10 | async-start | bytes 3276800 | tf_op jit(solution)/shard_map/all_gather | solution.py:152
  49.8 33.6 %copy-start.34 = (f32[40]{0:T(128)}, f32[40]{0:T(128)S(1)}, u32[]{:S(2)}) copy-start(f32[40]{0:T(128)S(1)} %get-tuple-element.100) | copy-start | bytes 484
  49.8 33.6 %copy-start.37 = (f32[40]{0:T(128)}, f32[40]{0:T(128)S(1)}, u32[]{:S(2)}) copy-start(f32[40]{0:T(128)S(1)} %get-tuple-element.102) | copy-start | bytes 484
  49.8 33.6 %copy-start.39 = (f32[40]{0:T(128)}, f32[40]{0:T(128)S(1)}, u32[]{:S(2)}) copy-start(f32[40]{0:T(128)S(1)} %get-tuple-element.101) | copy-start | bytes 484
  49.8 33.6 %copy-start.41 = (f32[40]{0:T(128)}, f32[40]{0:T(128)S(1)}, u32[]{:S(2)}) copy-start(f32[40]{0:T(128)S(1)} %get-tuple-element.103) | copy-start | bytes 484
  49.9 33.6 %copy-start.46 = (f32[40]{0:T(128)}, f32[40]{0:T(128)S(1)}, u32[]{:S(2)}) copy-start(f32[40]{0:T(128)S(1)} %get-tuple-element.99) | copy-start | bytes 484
  49.9 33.6 %copy-start.48 = (f32[40]{0:T(128)}, f32[40]{0:T(128)S(1)}, u32[]{:S(2)}) copy-start(f32[40]{0:T(128)S(1)} %get-tuple-element.104) | copy-start | bytes 484
  83.4 35.0 %all-to-all-start.3 = ((f32[8,40,8,128]{3,2,1,0:T(8,128)}), f32[8,40,8,128]{3,2,1,0:T(8,128)S(1)}, u32[]{:S(2)}, u32[]{:S(2)}) async-start(f32[8,40,8,128]{3,2,1,0:T(8,128)} %fusion.100), calls=%async_computation.3 | async-start | bytes 2621440 | tf_op jit(solution)/shard_map/all_to_all | solution.py:43
  119.5 35.4 %all-to-all-start = ((f32[4,256,640]{2,1,0:T(8,128)}), f32[4,256,640]{2,1,0:T(8,128)S(1)}, u32[]{:S(2)}, u32[]{:S(2)}) async-start(f32[4,256,640]{2,1,0:T(8,128)} %bitcast.338), calls=%async_computation | async-start | bytes 5242880 | tf_op jit(solution)/shard_map/all_to_all | solution.py:157
  123.8 54.2 %copy-start.14 = (f32[256,40]{0,1:T(8,128)}, f32[256,40]{0,1:T(8,128)S(1)}, u32[]{:S(2)}) copy-start(f32[256,40]{0,1:T(8,128)S(1)} %copy.227) | copy-start | bytes 122884
  129.4 27.9 %copy-start.26 = (pred[256,256]{1,0:T(8,128)(4,1)}, pred[256,256]{1,0:T(8,128)(4,1)S(1)}, u32[]{:S(2)}) copy-start(pred[256,256]{1,0:T(8,128)(4,1)S(1)} %iota_compare_fusion) | copy-start | bytes 196612
  130.7 26.6 %copy-start.16 = (f32[256,256]{1,0:T(8,128)}, f32[256,256]{1,0:T(8,128)S(1)}, u32[]{:S(2)}) copy-start(f32[256,256]{1,0:T(8,128)S(1)} %fusion.115) | copy-start | bytes 786436
  167.4 70.4 %copy-start.30 = (f32[256]{0:T(256)}, f32[256]{0:T(256)S(1)}, u32[]{:S(2)}) copy-start(f32[256]{0:T(256)S(1)} %get-tuple-element.106) | copy-start | bytes 3076
  169.4 21.6 %all-to-all-start.6 = ((bf16[256,4,640]{0,2,1:T(8,128)(2,1)}), bf16[256,4,640]{0,2,1:T(8,128)(2,1)}, u32[]{:S(2)}, u32[]{:S(2)}) async-start(bf16[256,4,640]{0,2,1:T(8,128)(2,1)} %multiply_convert_fusion), calls=%async_computation.6 | async-start | bytes 2621440 | tf_op jit(solution)/shard_map/all_to_all | solution.py:160
  191.0 35.6 %all-to-all-start.4 = ((f32[8,40,8,128]{3,2,1,0:T(8,128)}), f32[8,40,8,128]{3,2,1,0:T(8,128)}, u32[]{:S(2)}, u32[]{:S(2)}) async-start(f32[8,40,8,128]{3,2,1,0:T(8,128)} %copy.232), calls=%async_computation.4 | async-start | bytes 2621440 | tf_op jit(solution)/shard_map/all_to_all | solution.py:37
  226.6 42.5 %all-to-all-start.7 = ((bf16[8,80,1280]{2,1,0:T(8,128)(2,1)}), bf16[8,80,1280]{2,1,0:T(8,128)(2,1)}, u32[]{:S(2)}, u32[]{:S(2)}) async-start(bf16[8,80,1280]{2,1,0:T(8,128)(2,1)} %bitcast.340), calls=%async_computation.7 | async-start | bytes 3276800 | tf_op jit(solution)/shard_map/all_to_all | solution.py:165
  269.1 35.6 %all-to-all-start.5 = ((f32[8,40,8,128]{3,2,1,0:T(8,128)}), f32[8,40,8,128]{3,2,1,0:T(8,128)}, u32[]{:S(2)}, u32[]{:S(2)}) async-start(f32[8,40,8,128]{3,2,1,0:T(8,128)} %broadcast_dynamic-update-slice_fusion), calls=%async_computation.5 | async-start | bytes 2621440 | tf_op jit(solution)/shard_map/all_to_all | solution.py:43
  273.4 126.6 %all-gather.5.cloned.1.call-start = ((), (), s32[]{:S(2)}) async-start(), calls=%async_computation.9 | async-start | bytes 3686400 | tf_op jit(solution)/shard_map/all_gather | solution.py:173
  343.5 14.4 %all-to-all-start.8 = ((f32[32,1,640]{2,1,0:T(1,128)}), f32[32,1,640]{2,1,0:T(1,128)S(1)}, u32[]{:S(2)}, u32[]{:S(2)}) async-start(f32[32,1,640]{2,1,0:T(1,128)} %bitcast.102), calls=%async_computation.8 | async-start | bytes 163840 | tf_op jit(solution)/shard_map/all_to_all | solution.py:54
  350.3 6.3 %collective-permute-start.1 = (f32[3,2816]{1,0:T(4,128)S(1)}, f32[3,2816]{1,0:T(4,128)S(1)}, u32[]{:S(2)}, u32[]{:S(2)}) collective-permute-start(f32[3,2816]{1,0:T(4,128)S(1)} %pad_add_fusion.1), channel_id=1, source_target_pairs={{4,0},{8,4},{12,8},{16,12},{20,16},{24,20},{28,24},{5,1},{9,5},{13... | collective-permute-start | bytes 101384 | tf_op jit(solution)/shard_map/ppermute | solution.py:19
  (41 other events, 201.0 us)
Sparse Core Ops, SparseCore 0:
  49.4 26.9 all-gather.6
  304.8 62.9 all-gather.4
where the time goes:
time: 418 us; the launch traced here: 411 us
  waiting for transfers between devices  120 us (29%)
  other arithmetic  69.1 us (17%)
  matrix products  64.5 us (15%)
  local copies, waits for them, and re-layouts  54.6 us (13%)
  starting transfers between devices  47.2 us (11%)
  blocking collectives  40 us (10%)
  between operations  15.1 us (4%)
    all_to_all x2, waiting for transfers between devices, carried(): lax.all_to_all(pieces, axis, split_axis=0, concat_axis=0, tiled=True)  48.4 us
    all_gather x1, blocking collectives, summed_everywhere(): total = lax.all_gather(jnp.sum(terms, axis=0), axes, axis=0, tiled=True)  40 us
    dot_general x3, matrix products, finish(): inside = jnp.einsum('hcts,cshp->cthp', weights, scaled, precision=PRECISE)  30.7 us
    all_to_all x2, waiting for transfers between devices, carried(): lax.all_to_all(jnp.stack(found), axis, split_axis=0, concat_axis=0, tiled...  25.8 us
    all_to_all x1, waiting for transfers between devices, body(): lax.all_to_all(regrouped, 'dp', split_axis=0, concat_axis=2, tiled=True)  20.4 us
    unnamed x113, local copies, waits for them, and re-layouts  17.5 us
    all_to_all x1, waiting for transfers between devices, body(): lax.all_to_all(weight_piece.astype(jnp.bfloat16).reshape(spans, own_rows...  13.1 us
    unnamed x10, other arithmetic  12.2 us
  transfers between devices with their start and end apart: 13, of which 7 were waited for; matrix products, arithmetic and copies ran while one was open for 40% of the time, Pallas kernels for 0%

commit v1 on v0

--- a/solution.py
+++ b/solution.py
@@ -52,7 +52,10 @@
     chunk = -(-flat.shape[0] // (count * 128)) * 128
     padded = jnp.pad(flat, (0, chunk * count - flat.shape[0])).reshape(count, chunk)
     terms = lax.all_to_all(padded, axes, split_axis=0, concat_axis=0, tiled=True)
-    total = lax.all_gather(jnp.sum(terms, axis=0), axes, axis=0, tiled=True)
+    total = jnp.concatenate(
+        lax.all_to_all(jnp.stack([jnp.sum(terms, axis=0)] * lax.axis_size(axes)), axes, 0, 0),
+        axis=0,
+    )
     results, start = ([], 0)
     for part in parts:
         results.append(total[start : start + part.size].reshape(part.shape))

time: 418 us -> 391 us (0.935)
  blocking collectives: 40 us -> 0 us
  waiting for transfers between devices: 120 us -> 130 us
    all_gather x1 -> x0, blocking collectives: 40 us -> none  [summed_everywhere(): total = lax.all_gather(jnp.sum(terms, axis=0), axes, axis=0, tiled=True)]
    all_to_all x1, waiting for transfers between devices: 0.01 us -> 7.4 us  [summed_everywhere(): lax.all_to_all(padded, axes, split_axis=0, concat_axis=0, tiled=True)]
    all_to_all x0 -> x1, waiting for transfers between devices: none -> 5.81 us  [summed_everywhere(): lax.all_to_all(jnp.stack([jnp.sum(terms, axis=0)] * lax.axis_size(axes)),...]
    unnamed x113 -> x148, local copies, waits for them, and re-layouts: 17.5 us -> 17.5 us
  transfers between devices with their start and end apart: 13 -> 14, of which waited for: 7 -> 8; matrix products, arithmetic and copies ran while one was open for 40% -> 43% of each run, Pallas kernels for 0% -> 0%
where the time goes in v1:
time: 391 us; the launch traced here: 384 us
  waiting for transfers between devices  130 us (33%)
  other arithmetic  68.9 us (18%)
  matrix products  64.5 us (16%)
  local copies, waits for them, and re-layouts  55 us (14%)
  starting transfers between devices  50.6 us (13%)
  between operations  15.4 us (4%)
    all_to_all x2, waiting for transfers between devices, carried(): lax.all_to_all(pieces, axis, split_axis=0, concat_axis=0, tiled=True)  48.4 us
    dot_general x3, matrix products, finish(): inside = jnp.einsum('hcts,cshp->cthp', weights, scaled, precision=PRECISE)  30.7 us
    all_to_all x2, waiting for transfers between devices, carried(): lax.all_to_all(jnp.stack(found), axis, split_axis=0, concat_axis=0, tiled...  25.9 us
    all_to_all x1, waiting for transfers between devices, body(): lax.all_to_all(regrouped, 'dp', split_axis=0, concat_axis=2, tiled=True)  20.4 us
    unnamed x148, local copies, waits for them, and re-layouts  17.5 us
    all_to_all x1, waiting for transfers between devices, body(): lax.all_to_all(weight_piece.astype(jnp.bfloat16).reshape(spans, own_rows...  13 us
    unnamed x10, other arithmetic  12.3 us
    all_to_all x2, starting transfers between devices, carried(): lax.all_to_all(pieces, axis, split_axis=0, concat_axis=0, tiled=True)  10.3 us
  transfers between devices with their start and end apart: 14, of which 8 were waited for; matrix products, arithmetic and copies ran while one was open for 43% of the time, Pallas kernels for 0%

profile of v1, /device:TPU:0, one launch (start us, length us, event | category | flops | bytes accessed | tf_op | source)
XLA Modules:
  0.0 384.3 jit_solution(12091787677952692931)
XLA Ops:
  8.1 4.9 %collective-permute-start = (bf16[3,2816]{1,0:T(4,128)(2,1)S(1)}, bf16[3,2816]{1,0:T(4,128)(2,1)S(1)}, u32[]{:S(2)}, u32[]{:S(2)}) collective-permute-start(bf16[3,2816]{1,0:T(4,128)(2,1)S(1)} %slice_bitcast_fusion), channel_id=1, source_target_pairs={{0,4},{4,8},{8,12},{12,16},{16,20},{20,24},{24,28},{1,5},{5,9},{9,... | collective-permute-start | bytes 50696 | tf_op jit(solution)/shard_map/ppermute | solution.py:19
  16.9 4.9 %all-to-all-start.1 = ((f32[8,1,40]{2,1,0:T(1,128)}), f32[8,1,40]{2,1,0:T(1,128)S(1)}, u32[]{:S(2)}, u32[]{:S(2)}) async-start(f32[8,1,40]{2,1,0:T(1,128)} %broadcast_in_dim.32), calls=%async_computation.1 | async-start | bytes 8192 | tf_op jit(solution)/shard_map/all_to_all | solution.py:24
  41.2 6.0 %all-to-all-start.2 = ((f32[8,40,8,128]{3,2,1,0:T(8,128)}), f32[8,40,8,128]{3,2,1,0:T(8,128)S(1)}, u32[]{:S(2)}, u32[]{:S(2)}) async-start(f32[8,40,8,128]{3,2,1,0:T(8,128)} %copy.225), calls=%async_computation.2 | async-start | bytes 2621440 | tf_op jit(solution)/shard_map/all_to_all | solution.py:37
  50.0 28.0 %all-to-all-done.2 = f32[8,40,8,128]{3,2,1,0:T(8,128)S(1)} async-done(((f32[8,40,8,128]{3,2,1,0:T(8,128)}), f32[8,40,8,128]{3,2,1,0:T(8,128)S(1)}, u32[]{:S(2)}, u32[]{:S(2)}) %all-to-all-start.2) | async-done | bytes 1310752 | tf_op jit(solution)/shard_map/all_to_all | solution.py:37
  87.2 5.5 %fusion.44 = f32[1024,640]{1,0:T(8,128)} fusion(bf16[640,1280]{1,0:T(8,128)(2,1)S(1)} %copy-done, bf16[1,1024,1280]{2,1,0:T(8,128)(2,1)} %all-gather.6.cloned.1.call-done), kind=kOutput, calls=%fused_computation.67 | convolution fusion | flops 1677721600 | bytes 6881280 | tf_op jit(solution)/shard_map/dot_general | solution.py:156
  92.7 25.9 %all-to-all-done.3 = f32[8,40,8,128]{3,2,1,0:T(8,128)S(1)} async-done(((f32[8,40,8,128]{3,2,1,0:T(8,128)}), f32[8,40,8,128]{3,2,1,0:T(8,128)S(1)}, u32[]{:S(2)}, u32[]{:S(2)}) %all-to-all-start.3) | async-done | bytes 1310752 | tf_op jit(solution)/shard_map/all_to_all | solution.py:43
  134.6 20.4 %all-to-all-done = f32[4,256,640]{2,1,0:T(8,128)S(1)} async-done(((f32[4,256,640]{2,1,0:T(8,128)}), f32[4,256,640]{2,1,0:T(8,128)S(1)}, u32[]{:S(2)}, u32[]{:S(2)}) %all-to-all-start) | async-done | bytes 2621472 | tf_op jit(solution)/shard_map/all_to_all | solution.py:160
  157.5 10.2 %multiply_reduce_fusion.9 = (f32[256]{0:T(256)S(1)}, f32[256]{0:T(256)S(1)}, f32[1,256,40,64]{1,3,2,0:T(8,128)S(1)}) fusion(f32[1,256,40,64]{1,3,2,0:T(8,128)} %bitcast.316, f32[1,256,40,64]{1,3,2,0:T(8,128)} %bitcast.328, f32[40,64]{1,0:T(8,128)S(1)} %mul.692, f32[1,256,40,64]{1,3,2,0:T(8,128)} %bitcast.322, f32[40]{0:T(128)S(1)} %copy-done.68, ...), kind=kOutput, calls=%fused_computation.74 | convolution fusion | flops 1024327168 | bytes 16191648 | tf_op jit(solution)/shard_map/jvp(hcts,cshp->cthp)/dot_general | solution.py:101
  169.6 4.3 %all-to-all-start.6 = ((bf16[256,4,640]{0,2,1:T(8,128)(2,1)}), bf16[256,4,640]{0,2,1:T(8,128)(2,1)}, u32[]{:S(2)}, u32[]{:S(2)}) async-start(bf16[256,4,640]{0,2,1:T(8,128)(2,1)} %multiply_convert_fusion), calls=%async_computation.6 | async-start | bytes 2621440 | tf_op jit(solution)/shard_map/all_to_all | solution.py:163
  182.9 8.3 %all-to-all-done.6 = bf16[256,4,640]{0,2,1:T(8,128)(2,1)} async-done(((bf16[256,4,640]{0,2,1:T(8,128)(2,1)}), bf16[256,4,640]{0,2,1:T(8,128)(2,1)}, u32[]{:S(2)}, u32[]{:S(2)}) %all-to-all-start.6) | async-done | bytes 1310752 | tf_op jit(solution)/shard_map/all_to_all | solution.py:163
  191.2 4.3 %all-to-all-start.4 = ((f32[8,40,8,128]{3,2,1,0:T(8,128)}), f32[8,40,8,128]{3,2,1,0:T(8,128)}, u32[]{:S(2)}, u32[]{:S(2)}) async-start(f32[8,40,8,128]{3,2,1,0:T(8,128)} %copy.232), calls=%async_computation.4 | async-start | bytes 2621440 | tf_op jit(solution)/shard_map/all_to_all | solution.py:37
  201.2 5.2 %convolution_convert_fusion = bf16[640,1280]{1,0:T(8,128)(2,1)} fusion(bf16[1024,640]{1,0:T(8,128)(2,1)} %bitcast.341, bf16[1,1024,1280]{2,1,0:T(8,128)(2,1)} %all-gather.6.cloned.1.call-done), kind=kOutput, calls=%fused_computation.24 | convolution fusion | flops 1678540800 | bytes 5570560 | tf_op jit(solution)/shard_map/dot_general | solution.py:164
  206.4 20.5 %all-to-all-done.4 = f32[8,40,8,128]{3,2,1,0:T(8,128)} async-done(((f32[8,40,8,128]{3,2,1,0:T(8,128)}), f32[8,40,8,128]{3,2,1,0:T(8,128)}, u32[]{:S(2)}, u32[]{:S(2)}) %all-to-all-start.4) | async-done | bytes 1310752 | tf_op jit(solution)/shard_map/all_to_all | solution.py:37
  226.9 4.5 %all-to-all-start.7 = ((bf16[8,80,1280]{2,1,0:T(8,128)(2,1)}), bf16[8,80,1280]{2,1,0:T(8,128)(2,1)}, u32[]{:S(2)}, u32[]{:S(2)}) async-start(bf16[8,80,1280]{2,1,0:T(8,128)(2,1)} %bitcast.339), calls=%async_computation.7 | async-start | bytes 3276800 | tf_op jit(solution)/shard_map/all_to_all | solution.py:168
  231.4 4.4 %fusion.24 = bf16[1,256,2560]{1,2,0:T(8,128)(2,1)} fusion(f32[1,256,4,640]{1,3,2,0:T(8,128)} %copy.218, f32[1,256,40,64]{1,3,2,0:T(8,128)S(1)} %get-tuple-element.108, f32[256]{0:T(256)S(1)} %get-tuple-element.107, f32[256]{0:T(256)S(1)} %get-tuple-element.106, f32[2560]{0:T(1024)S(1)} %copy-done.36, bf16[1,256,2560]{1,2,0:T(8,128)(2,1)} %copy.229), kind=kLoop, calls=%fused_computation.40 | loop fusion | flops 12451840 | bytes 7876608 | tf_op jit(solution)/shard_map/convert_element_type | solution.py:212
  256.4 13.0 %all-to-all-done.7 = bf16[8,80,1280]{2,1,0:T(8,128)(2,1)} async-done(((bf16[8,80,1280]{2,1,0:T(8,128)(2,1)}), bf16[8,80,1280]{2,1,0:T(8,128)(2,1)}, u32[]{:S(2)}, u32[]{:S(2)}) %all-to-all-start.7) | async-done | bytes 1638432 | tf_op jit(solution)/shard_map/all_to_all | solution.py:168
  269.4 4.3 %all-to-all-start.5 = ((f32[8,40,8,128]{3,2,1,0:T(8,128)}), f32[8,40,8,128]{3,2,1,0:T(8,128)}, u32[]{:S(2)}, u32[]{:S(2)}) async-start(f32[8,40,8,128]{3,2,1,0:T(8,128)} %broadcast_dynamic-update-slice_fusion), calls=%async_computation.5 | async-start | bytes 2621440 | tf_op jit(solution)/shard_map/all_to_all | solution.py:43
  273.7 13.1 %fusion.6 = (f32[40,256]{1,0:T(8,128)}, f32[40,256]{1,0:T(8,128)S(1)}, f32[256,256]{1,0:T(8,128)S(1)}) fusion(f32[40,256]{1,0:T(8,128)} %get-tuple-element.88, f32[256,256]{1,0:T(8,128)S(1)} %copy-done.23, pred[256,256]{1,0:T(8,128)(4,1)} %copy-done.37, f32[256,40,64]{0,2,1:T(8,128)} %bitcast.324, f32[256,40]{0,1:T(8,128)S(1)} %fusion.124, ...), kind=kOutput, calls=%fused_computation.7 | convolution fusion | flops 1030795264 | bytes 5996544 | tf_op jit(solution)/shard_map/transpose(jvp(hcts,cshp->cthp))/dot_general | solution.py:101
  291.3 4.4 %multiply_reduce_fusion.6 = f32[4,640]{1,0:T(4,128)S(1)} fusion(f32[1,256,4,640]{3,1,2,0:T(8,128)} %copy.248, f32[1,256,4,640]{3,1,2,0:T(8,128)} %copy.247, f32[256]{0:T(256)S(1)} %copy-done.43, f32[4,256,640]{2,1,0:T(8,128)} %copy-done.9), kind=kLoop, calls=%fused_computation.70 | loop fusion | flops 5240320 | bytes 7875584 | tf_op jit(solution)/shard_map/transpose(jvp())/reduce_sum | solution.py:110
  311.7 7.5 %multiply_reduce_fusion.5 = (f32[40]{0:T(128)}, f32[256,40]{0,1:T(8,128)}, f32[1,256,40,64]{1,3,2,0:T(8,128)}) fusion(f32[1,256,40,64]{1,3,2,0:T(8,128)S(1)} %copy-done.12, f32[1,256,40,64]{1,3,2,0:T(8,128)S(1)} %bitcast.326, f32[256,40]{0,1:T(8,128)S(1)} %fusion.124, f32[256,40]{0,1:T(8,128)S(1)} %get-tuple-element.87, ...), kind=kOutput, calls=%fused_computation.69 | convolution fusion | flops 1019074560 | bytes 10977440 | tf_op jit(solution)/shard_map/transpose(jvp(hcts,cshp->cthp))/dot_general | solution.py:101
  326.2 6.0 %multiply_reduce_fusion.4 = (f32[2816]{0:T(1024)S(1)}, f32[2816]{0:T(1024)S(1)}, f32[2816]{0:T(1024)S(1)}, f32[2816]{0:T(1024)S(1)}, f32[2816]{0:T(1024)S(1)}, /*index=5*/f32[256,2816]{1,0:T(8,128)}) fusion(f32[259,2816]{1,0:T(8,128)S(1)} %copy-done.3, f32[256,2816]{1,0:T(8,128)} %get-tuple-element.90, f32[256,2560]{1,0:T(8,128)} %copy.235, ...), kind=kLoop, calls=%fused_computation.32 | loop fusion | flops 15845632 | bytes 22993920 | tf_op jit(solution)/shard_map/transpose(jvp())/reduce_sum | solution.py:71
  345.1 5.7 %all-to-all-start.8 = ((f32[32,1,640]{2,1,0:T(1,128)}), f32[32,1,640]{2,1,0:T(1,128)S(1)}, u32[]{:S(2)}, u32[]{:S(2)}) async-start(f32[32,1,640]{2,1,0:T(1,128)} %bitcast.102), calls=%async_computation.8 | async-start | bytes 163840 | tf_op jit(solution)/shard_map/all_to_all | solution.py:54
  351.8 7.4 %all-to-all-done.8 = f32[32,1,640]{2,1,0:T(1,128)S(1)} async-done(((f32[32,1,640]{2,1,0:T(1,128)}), f32[32,1,640]{2,1,0:T(1,128)S(1)}, u32[]{:S(2)}, u32[]{:S(2)}) %all-to-all-start.8) | async-done | bytes 81952 | tf_op jit(solution)/shard_map/all_to_all | solution.py:54
  365.1 5.8 %all-to-all-done.9 = f32[32,1,640]{2,1,0:T(1,128)S(1)} async-done(((f32[32,1,640]{2,1,0:T(1,128)}), f32[32,1,640]{2,1,0:T(1,128)S(1)}, u32[]{:S(2)}, u32[]{:S(2)}) %all-to-all-start.9) | async-done | bytes 81952 | tf_op jit(solution)/shard_map/all_to_all | solution.py:56
  (274 shorter events, 144.7 us)
Async XLA Ops:
  7.2 80.0 %copy-start = (bf16[640,1280]{1,0:T(8,128)(2,1)S(1)}, bf16[640,1280]{1,0:T(8,128)(2,1)}, u32[]{:S(2)}) copy-start(bf16[640,1280]{1,0:T(8,128)(2,1)} %param.20) | copy-start | bytes 4915204
  8.1 16.9 %collective-permute-start = (bf16[3,2816]{1,0:T(4,128)(2,1)S(1)}, bf16[3,2816]{1,0:T(4,128)(2,1)S(1)}, u32[]{:S(2)}, u32[]{:S(2)}) collective-permute-start(bf16[3,2816]{1,0:T(4,128)(2,1)S(1)} %slice_bitcast_fusion), channel_id=1, source_target_pairs={{0,4},{4,8},{8,12},{12,16},{16,20},{20,24},{24,28},{1,5},{5,9},{9,... | collective-permute-start | bytes 50696 | tf_op jit(solution)/shard_map/ppermute | solution.py:19
  16.9 23.7 %all-to-all-start.1 = ((f32[8,1,40]{2,1,0:T(1,128)}), f32[8,1,40]{2,1,0:T(1,128)S(1)}, u32[]{:S(2)}, u32[]{:S(2)}) async-start(f32[8,1,40]{2,1,0:T(1,128)} %broadcast_in_dim.32), calls=%async_computation.1 | async-start | bytes 8192 | tf_op jit(solution)/shard_map/all_to_all | solution.py:24
  41.2 36.8 %all-to-all-start.2 = ((f32[8,40,8,128]{3,2,1,0:T(8,128)}), f32[8,40,8,128]{3,2,1,0:T(8,128)S(1)}, u32[]{:S(2)}, u32[]{:S(2)}) async-start(f32[8,40,8,128]{3,2,1,0:T(8,128)} %copy.225), calls=%async_computation.2 | async-start | bytes 2621440 | tf_op jit(solution)/shard_map/all_to_all | solution.py:37
  47.2 40.0 %all-gather.6.cloned.1.call-start = ((), (), s32[]{:S(2)}) async-start(), calls=%async_computation.11 | async-start | bytes 3276800 | tf_op jit(solution)/shard_map/all_gather | solution.py:155
  50.0 33.6 %copy-start.46 = (f32[40]{0:T(128)}, f32[40]{0:T(128)S(1)}, u32[]{:S(2)}) copy-start(f32[40]{0:T(128)S(1)} %get-tuple-element.100) | copy-start | bytes 484
  50.0 33.6 %copy-start.49 = (f32[40]{0:T(128)}, f32[40]{0:T(128)S(1)}, u32[]{:S(2)}) copy-start(f32[40]{0:T(128)S(1)} %get-tuple-element.102) | copy-start | bytes 484
  50.0 33.6 %copy-start.51 = (f32[40]{0:T(128)}, f32[40]{0:T(128)S(1)}, u32[]{:S(2)}) copy-start(f32[40]{0:T(128)S(1)} %get-tuple-element.101) | copy-start | bytes 484
  50.0 33.6 %copy-start.53 = (f32[40]{0:T(128)}, f32[40]{0:T(128)S(1)}, u32[]{:S(2)}) copy-start(f32[40]{0:T(128)S(1)} %get-tuple-element.103) | copy-start | bytes 484
  50.0 33.6 %copy-start.60 = (f32[40]{0:T(128)}, f32[40]{0:T(128)S(1)}, u32[]{:S(2)}) copy-start(f32[40]{0:T(128)S(1)} %get-tuple-element.99) | copy-start | bytes 484
  50.0 33.6 %copy-start.62 = (f32[40]{0:T(128)}, f32[40]{0:T(128)S(1)}, u32[]{:S(2)}) copy-start(f32[40]{0:T(128)S(1)} %get-tuple-element.104) | copy-start | bytes 484
  83.6 35.0 %all-to-all-start.3 = ((f32[8,40,8,128]{3,2,1,0:T(8,128)}), f32[8,40,8,128]{3,2,1,0:T(8,128)S(1)}, u32[]{:S(2)}, u32[]{:S(2)}) async-start(f32[8,40,8,128]{3,2,1,0:T(8,128)} %fusion.100), calls=%async_computation.3 | async-start | bytes 2621440 | tf_op jit(solution)/shard_map/all_to_all | solution.py:43
  119.6 35.4 %all-to-all-start = ((f32[4,256,640]{2,1,0:T(8,128)}), f32[4,256,640]{2,1,0:T(8,128)S(1)}, u32[]{:S(2)}, u32[]{:S(2)}) async-start(f32[4,256,640]{2,1,0:T(8,128)} %bitcast.337), calls=%async_computation | async-start | bytes 5242880 | tf_op jit(solution)/shard_map/all_to_all | solution.py:160
  123.9 54.3 %copy-start.20 = (f32[256,40]{0,1:T(8,128)}, f32[256,40]{0,1:T(8,128)S(1)}, u32[]{:S(2)}) copy-start(f32[256,40]{0,1:T(8,128)S(1)} %copy.227) | copy-start | bytes 122884
  129.5 27.9 %copy-start.37 = (pred[256,256]{1,0:T(8,128)(4,1)}, pred[256,256]{1,0:T(8,128)(4,1)S(1)}, u32[]{:S(2)}) copy-start(pred[256,256]{1,0:T(8,128)(4,1)S(1)} %iota_compare_fusion) | copy-start | bytes 196612
  167.7 70.5 %copy-start.42 = (f32[256]{0:T(256)}, f32[256]{0:T(256)S(1)}, u32[]{:S(2)}) copy-start(f32[256]{0:T(256)S(1)} %get-tuple-element.106) | copy-start | bytes 3076
  169.6 21.6 %all-to-all-start.6 = ((bf16[256,4,640]{0,2,1:T(8,128)(2,1)}), bf16[256,4,640]{0,2,1:T(8,128)(2,1)}, u32[]{:S(2)}, u32[]{:S(2)}) async-start(bf16[256,4,640]{0,2,1:T(8,128)(2,1)} %multiply_convert_fusion), calls=%async_computation.6 | async-start | bytes 2621440 | tf_op jit(solution)/shard_map/all_to_all | solution.py:163
  191.2 35.6 %all-to-all-start.4 = ((f32[8,40,8,128]{3,2,1,0:T(8,128)}), f32[8,40,8,128]{3,2,1,0:T(8,128)}, u32[]{:S(2)}, u32[]{:S(2)}) async-start(f32[8,40,8,128]{3,2,1,0:T(8,128)} %copy.232), calls=%async_computation.4 | async-start | bytes 2621440 | tf_op jit(solution)/shard_map/all_to_all | solution.py:37
  226.9 42.5 %all-to-all-start.7 = ((bf16[8,80,1280]{2,1,0:T(8,128)(2,1)}), bf16[8,80,1280]{2,1,0:T(8,128)(2,1)}, u32[]{:S(2)}, u32[]{:S(2)}) async-start(bf16[8,80,1280]{2,1,0:T(8,128)(2,1)} %bitcast.339), calls=%async_computation.7 | async-start | bytes 3276800 | tf_op jit(solution)/shard_map/all_to_all | solution.py:168
  269.4 35.6 %all-to-all-start.5 = ((f32[8,40,8,128]{3,2,1,0:T(8,128)}), f32[8,40,8,128]{3,2,1,0:T(8,128)}, u32[]{:S(2)}, u32[]{:S(2)}) async-start(f32[8,40,8,128]{3,2,1,0:T(8,128)} %broadcast_dynamic-update-slice_fusion), calls=%async_computation.5 | async-start | bytes 2621440 | tf_op jit(solution)/shard_map/all_to_all | solution.py:43
  273.7 99.7 %all-gather.4.cloned.1.call-start = ((), (), s32[]{:S(2)}) async-start(), calls=%async_computation.10 | async-start | bytes 3686400 | tf_op jit(solution)/shard_map/all_gather | solution.py:176
  338.9 12.0 %collective-permute-start.1 = (f32[3,2816]{1,0:T(4,128)S(1)}, f32[3,2816]{1,0:T(4,128)S(1)}, u32[]{:S(2)}, u32[]{:S(2)}) collective-permute-start(f32[3,2816]{1,0:T(4,128)S(1)} %pad_add_fusion.1), channel_id=1, source_target_pairs={{4,0},{8,4},{12,8},{16,12},{20,16},{24,20},{28,24},{5,1},{9,5},{13... | collective-permute-start | bytes 101384 | tf_op jit(solution)/shard_map/ppermute | solution.py:19
  345.1 14.1 %all-to-all-start.8 = ((f32[32,1,640]{2,1,0:T(1,128)}), f32[32,1,640]{2,1,0:T(1,128)S(1)}, u32[]{:S(2)}, u32[]{:S(2)}) async-start(f32[32,1,640]{2,1,0:T(1,128)} %bitcast.102), calls=%async_computation.8 | async-start | bytes 163840 | tf_op jit(solution)/shard_map/all_to_all | solution.py:54
  360.0 10.9 %all-to-all-start.9 = ((f32[32,1,640]{2,1,0:T(1,128)}), f32[32,1,640]{2,1,0:T(1,128)S(1)}, u32[]{:S(2)}, u32[]{:S(2)}) async-start(f32[32,1,640]{2,1,0:T(1,128)} %stack.20), calls=%async_computation.9 | async-start | bytes 163840 | tf_op jit(solution)/shard_map/all_to_all | solution.py:56
  (60 other events, 305.3 us)
Sparse Core Ops, SparseCore 0:
  49.6 26.9 all-gather.5
  305.1 66.0 all-gather.3
